TPU v7x, 512 devices: a whole 4x4x16 slice. The times are simulated.
512 devices in a mesh: lon: 32 (over z_lo, y), lat: 16 (over z_hi, x, core).
Axes of the slice: x: 4, y: 4, z: 16 (z_hi: 2, z_lo: 8; z = z_hi * 8 + z_lo), core: 2. Of those that a mesh axis runs over, the one named last changes fastest.
Arguments:
- fields: bfloat16 [16, 64, 32, 4096], P('lat', None, None, 'lon'), may hold values from -40 to 40
- ocean_mask: int32 [16, 32, 4096], P('lat', None, 'lon'), may hold values 0 or 1
- norm_gain: float32 [64], replicated, may hold values from 0.5 to 1.5
- w_vert: bfloat16 [5, 8, 8, 8], replicated, may hold values from -1 to 1
- b_vert: float32 [64], replicated, may hold values from -3 to 3
- w_horiz: bfloat16 [5, 64, 5, 64], replicated, may hold values from -0.15625 to 0.15625
- b_horiz: float32 [64], replicated, may hold values from -3 to 3
Outputs:
- updated: bfloat16 [16, 64, 32, 4096], P('lat', None, None, 'lon')
All inputs are finite; a program needn't handle non-finite values. No bound on the sum of `ocean_mask` on one device may be relied on, other than what follows from the above.
Results may differ from a plain program's by a relative error of at most 0.0023.
Values may be sent and summed in bfloat16 or wider, within the bound.
A program may use at most 64 MiB of HBM per device.

v0:
```python
import jax
import jax.numpy as jnp
from jax import lax
from jax.sharding import PartitionSpec as P


def extended_2(shard, sides, width):
    for axis, dim in sides:
        devices, length = (lax.axis_size(axis), shard.shape[dim])
        up = [(i, (i + 1) % devices) for i in range(devices)]
        down = [(j, i) for i, j in up]
        last = lax.slice_in_dim(shard, length - width, length, axis=dim)
        leading = lax.slice_in_dim(shard, 0, width, axis=dim)
        before = lax.ppermute(last, axis, up)
        after = lax.ppermute(leading, axis, down)
        shard = jnp.concatenate([before, shard, after], axis=dim)
    return shard


def normalize(block, norm_gain):
    values = block.astype(jnp.float32)
    center = jnp.mean(values, axis=1, keepdims=True)
    spread = jnp.mean((values - center) ** 2, axis=1, keepdims=True)
    return ((values - center) * lax.rsqrt(spread + 1e-05) * norm_gain[None, :, None, None]).astype(
        jnp.bfloat16
    )


def vertical(taps, w_vert, b_vert):
    count_lev, channels, rows_lat, cols_lon = taps[0].shape
    groups, width_in, width_out = (w_vert.shape[1], w_vert.shape[2], w_vert.shape[3])
    summed = jnp.zeros((count_lev, groups, width_out, rows_lat, cols_lon), jnp.float32)
    for tap_index in range(len(taps)):
        grouped = taps[tap_index].reshape(count_lev, groups, width_in, rows_lat, cols_lon)
        summed = summed + jnp.einsum(
            "gio,ngiab->ngoab", w_vert[tap_index], grouped, preferred_element_type=jnp.float32
        )
    summed = summed.reshape(count_lev, channels, rows_lat, cols_lon) + b_vert[None, :, None, None]
    return jax.nn.gelu(summed).astype(jnp.bfloat16)


def shifted(block, axis, offset):
    devices = lax.axis_size(axis)
    pairs = [(i, i - offset) for i in range(devices) if 0 <= i - offset < devices]
    return lax.ppermute(block, axis, pairs)


def lon_halo(block, width):
    devices = lax.axis_size("lon")
    length = block.shape[-1]
    up = [(i, (i + 1) % devices) for i in range(devices)]
    down = [(j, i) for i, j in up]
    before = lax.ppermute(block[..., length - width :], "lon", up)
    after = lax.ppermute(block[..., :width], "lon", down)
    return (before, after)


def local(fields, ocean_mask, norm_gain, w_vert, b_vert, w_horiz, b_horiz):
    reach = w_vert.shape[0] // 2
    lat = ("lat_hi", "lat_lo")
    field_before, field_after = lon_halo(fields, reach)
    mask_before, mask_after = lon_halo(ocean_mask, reach)
    halo = jnp.concatenate([field_before, field_after], axis=3)
    halo_normed = normalize(halo, norm_gain)
    halo_taps = [
        halo_normed if tap == reach else shifted(halo_normed, lat, tap - reach)
        for tap in range(w_vert.shape[0])
    ]
    halo_mask = jnp.concatenate([mask_before, mask_after], axis=2)
    halo_masked = vertical(halo_taps, w_vert, b_vert) * halo_mask[:, None].astype(jnp.bfloat16)
    normed = normalize(fields, norm_gain)
    columns = lax.all_to_all(normed, "lat_lo", split_axis=2, concat_axis=0, tiled=True)
    count_lev = columns.shape[0]
    upper = lax.axis_index("lat_hi") == 0
    send = jnp.where(upper, columns[count_lev - reach :], columns[:reach])
    recv = lax.ppermute(send, "lat_hi", [(0, 1), (1, 0)])
    zeros = jnp.zeros_like(recv)
    below = jnp.where(upper, zeros, recv)
    above = jnp.where(upper, recv, zeros)
    padded = jnp.concatenate([below, columns, above], axis=0)
    taps = [padded[tap_index : tap_index + count_lev] for tap_index in range(w_vert.shape[0])]
    mixed = lax.all_to_all(
        vertical(taps, w_vert, b_vert), "lat_lo", split_axis=0, concat_axis=2, tiled=True
    )
    masked = mixed * ocean_mask[:, None].astype(jnp.bfloat16)
    extended = jnp.concatenate([halo_masked[..., :reach], masked, halo_masked[..., reach:]], axis=3)
    extended = jnp.pad(extended, ((0, 0), (0, 0), (2, 2), (0, 0)))
    channels, rows_lat, cols_lon = (masked.shape[1], masked.shape[2], masked.shape[3])
    summed = jnp.zeros(masked.shape, jnp.float32)
    for row_tap in range(w_horiz.shape[0]):
        stacked = jnp.concatenate(
            [
                extended[:, :, row_tap : row_tap + rows_lat, col_tap : col_tap + cols_lon]
                for col_tap in range(w_horiz.shape[2])
            ],
            axis=1,
        )
        kernel = w_horiz[row_tap].reshape(channels, -1)
        summed = summed + jnp.einsum(
            "oj,njab->noab", kernel, stacked, preferred_element_type=jnp.float32
        )
    ocean = ocean_mask[:, None].astype(jnp.float32)
    return (fields.astype(jnp.float32) + ocean * (summed + b_horiz[None, :, None, None])).astype(
        jnp.bfloat16
    )


def solution(mesh):
    halves = 2
    lon_count, lat_count = mesh.devices.shape
    split = jax.sharding.Mesh(
        mesh.devices.reshape(lon_count, halves, lat_count // halves), ("lon", "lat_hi", "lat_lo")
    )
    lat = ("lat_hi", "lat_lo")
    placed = (P(lat, None, None, "lon"), P(lat, None, "lon"), P(), P(), P(), P(), P())
    return jax.shard_map(
        local, mesh=split, in_specs=placed, out_specs=P(lat, None, None, "lon"), check_vma=False
    )
```

profile of v0, /device:TPU:1, one launch (start us, length us, event | category | flops | bytes accessed | tf_op | source)
XLA Modules:
  0.0 129.0 jit_solution(12597623093102594426)
XLA Ops:
  0.0 0.9 fusion.130
  0.9 16.2 %collective-permute-start.7 = (s32[1,32,2]{1,2,0:T(2,128)S(1)}, s32[1,32,2]{1,2,0:T(2,128)S(1)}, u32[]{:S(2)}, u32[]{:S(2)}) collective-permute-start(s32[1,32,2]{1,2,0:T(2,128)S(1)} %copy.167), channel_id=1, source_target_pairs={{16,0},{32,16},{48,32},{64,48},{80,64},{96,80},{112,96},{128,112},... | collective-permute-start | bytes 776 | tf_op jit(solution)/shard_map/ppermute | solution.py:54
  17.1 0.1 copy.166
  17.2 1.9 %collective-permute-start.6 = (s32[1,32,2]{1,2,0:T(2,128)S(1)}, s32[1,32,2]{1,2,0:T(2,128)S(1)}, u32[]{:S(2)}, u32[]{:S(2)}) collective-permute-start(s32[1,32,2]{1,2,0:T(2,128)S(1)} %copy.166), channel_id=1, source_target_pairs={{0,16},{16,32},{32,48},{48,64},{64,80},{80,96},{96,112},{112,128},... | collective-permute-start | bytes 776 | tf_op jit(solution)/shard_map/ppermute | solution.py:53
  19.1 1.2 convert_reduce_fusion
  20.3 1.3 fusion.51
  21.7 2.2 %fusion.70 = bf16[1,64,32,128]{3,1,0,2:T(8,128)(2,1)} fusion(f32[64]{0:T(128)} %param.9, f32[32,128]{1,0:T(8,128)S(1)} %add_rsqrt_fusion, f32[32,128]{1,0:T(8,128)S(1)} %broadcast_multiply_fusion, bf16[1,64,32,128]{3,2,1,0:T(8,128)(2,1)} %param.7), kind=kLoop, calls=%fused_computation.71 | loop fusion | flops 1310720 | bytes 1081600 | tf_op jit(solution)/shard_map/convert_element_type | solution.py:24
  23.9 5.3 %all-to-all-start = ((bf16[1,64,32,128]{3,1,0,2:T(8,128)(2,1)}), bf16[1,64,32,128]{3,1,0,2:T(8,128)(2,1)S(1)}, u32[]{:S(2)}, u32[]{:S(2)}) async-start(bf16[1,64,32,128]{3,1,0,2:T(8,128)(2,1)} %fusion.70), calls=%async_computation | async-start | bytes 1048576 | tf_op jit(solution)/shard_map/all_to_all | solution.py:72
  29.1 0.2 fusion.127
  29.4 0.5 copy.160
  29.8 12.4 %collective-permute-start.1 = (bf16[1,64,32,2]{2,1,3,0:T(8,128)(2,1)S(1)}, bf16[1,64,32,2]{2,1,3,0:T(8,128)(2,1)S(1)}, u32[]{:S(2)}, u32[]{:S(2)}) collective-permute-start(bf16[1,64,32,2]{2,1,3,0:T(8,128)(2,1)S(1)} %copy.160), channel_id=1, source_target_pairs={{16,0},{32,16},{48,32},{64,48},{80,64},{96,80},{112,96},{128,112},... | collective-permute-start | bytes 24584 | tf_op jit(solution)/shard_map/ppermute | solution.py:54
  42.2 0.5 copy.159
  42.7 1.9 %collective-permute-start = (bf16[1,64,32,2]{2,1,3,0:T(8,128)(2,1)S(1)}, bf16[1,64,32,2]{2,1,3,0:T(8,128)(2,1)S(1)}, u32[]{:S(2)}, u32[]{:S(2)}) collective-permute-start(bf16[1,64,32,2]{2,1,3,0:T(8,128)(2,1)S(1)} %copy.159), channel_id=1, source_target_pairs={{0,16},{16,32},{32,48},{48,64},{64,80},{80,96},{96,112},{112,128},... | collective-permute-start | bytes 24584 | tf_op jit(solution)/shard_map/ppermute | solution.py:53
  44.6 0.1 mul.183
  44.8 0.1 copy.125
  44.9 0.1 copy.131
  45.0 0.1 copy.127
  45.2 0.1 copy.135
  45.3 0.1 copy.133
  45.5 12.0 %collective-permute-done = bf16[1,64,32,2]{2,1,3,0:T(8,128)(2,1)S(1)} collective-permute-done((bf16[1,64,32,2]{2,1,3,0:T(8,128)(2,1)S(1)}, bf16[1,64,32,2]{2,1,3,0:T(8,128)(2,1)S(1)}, u32[]{:S(2)}, u32[]{:S(2)}) %collective-permute-start) | collective-permute-done | bytes 8224 | tf_op jit(solution)/shard_map/ppermute | solution.py:53
  57.5 0.1 fusion.85
  57.6 1.3 %collective-permute-start.5 = (bf16[1,64,32,4]{2,1,3,0:T(8,128)(2,1)S(1)}, bf16[1,64,32,4]{2,1,3,0:T(8,128)(2,1)S(1)}, u32[]{:S(2)}, u32[]{:S(2)}) collective-permute-start(bf16[1,64,32,4]{2,1,3,0:T(8,128)(2,1)S(1)} %fusion.85), channel_id=1, source_target_pairs={{2,0},{3,1},{4,2},{5,3},{6,4},{7,5},{8,6},{9,7},{10,8},{11,9},{12,... | collective-permute-start | bytes 49160 | tf_op jit(solution)/shard_map/ppermute | solution.py:45
  58.9 3.8 %collective-permute-start.4 = (bf16[1,64,32,4]{2,1,3,0:T(8,128)(2,1)S(1)}, bf16[1,64,32,4]{2,1,3,0:T(8,128)(2,1)S(1)}, u32[]{:S(2)}, u32[]{:S(2)}) collective-permute-start(bf16[1,64,32,4]{2,1,3,0:T(8,128)(2,1)S(1)} %fusion.85), channel_id=1, source_target_pairs={{1,0},{2,1},{3,2},{4,3},{5,4},{6,5},{7,6},{8,7},{9,8},{10,9},{11,1... | collective-permute-start | bytes 49160 | tf_op jit(solution)/shard_map/ppermute | solution.py:45
  62.7 4.2 %collective-permute-start.3 = (bf16[1,64,32,4]{2,1,3,0:T(8,128)(2,1)S(1)}, bf16[1,64,32,4]{2,1,3,0:T(8,128)(2,1)S(1)}, u32[]{:S(2)}, u32[]{:S(2)}) collective-permute-start(bf16[1,64,32,4]{2,1,3,0:T(8,128)(2,1)S(1)} %fusion.85), channel_id=1, source_target_pairs={{0,1},{1,2},{2,3},{3,4},{4,5},{5,6},{6,7},{7,8},{8,9},{9,10},{10,1... | collective-permute-start | bytes 49160 | tf_op jit(solution)/shard_map/ppermute | solution.py:45
  66.9 2.0 %collective-permute-start.2 = (bf16[1,64,32,4]{2,1,3,0:T(8,128)(2,1)S(1)}, bf16[1,64,32,4]{2,1,3,0:T(8,128)(2,1)S(1)}, u32[]{:S(2)}, u32[]{:S(2)}) collective-permute-start(bf16[1,64,32,4]{2,1,3,0:T(8,128)(2,1)S(1)} %fusion.85), channel_id=1, source_target_pairs={{0,2},{1,3},{2,4},{3,5},{4,6},{5,7},{6,8},{7,9},{8,10},{9,11},{10,... | collective-permute-start | bytes 49160 | tf_op jit(solution)/shard_map/ppermute | solution.py:45
  68.9 0.2 fusion.95
  69.2 0.2 fusion.100
  69.4 0.9 collective-permute-done.2
  70.2 0.2 fusion.50
  70.5 26.1 %collective-permute-start.8 = (bf16[2,64,4,128]{3,1,2,0:T(8,128)(2,1)S(1)}, bf16[2,64,4,128]{3,1,2,0:T(8,128)(2,1)S(1)}, u32[]{:S(2)}, u32[]{:S(2)}) collective-permute-start(bf16[2,64,4,128]{3,1,2,0:T(8,128)(2,1)S(1)} %fusion.86), channel_id=1, source_target_pairs={{0,8},{8,0},{1,9},{9,1},{2,10},{10,2},{3,11},{11,3},{4,12},{12,4},... | collective-permute-start | bytes 393224 | tf_op jit(solution)/shard_map/ppermute | solution.py:76
  96.6 0.2 fusion.97
  96.8 3.3 %collective-permute-done.8 = bf16[2,64,4,128]{3,1,2,0:T(8,128)(2,1)S(1)} collective-permute-done((bf16[2,64,4,128]{3,1,2,0:T(8,128)(2,1)S(1)}, bf16[2,64,4,128]{3,1,2,0:T(8,128)(2,1)S(1)}, u32[]{:S(2)}, u32[]{:S(2)}) %collective-permute-start.8) | collective-permute-done | bytes 131104 | tf_op jit(solution)/shard_map/ppermute | solution.py:76
  100.1 0.1 fusion.73
  100.3 0.3 fusion.79
  100.6 0.4 convolution_add_fusion.3
  101.0 0.3 convolution_add_fusion.2
  101.4 0.4 convolution_add_fusion.1
  101.7 0.4 fusion.26
  102.1 1.2 fusion.61
  103.3 4.3 %all-to-all-start.1 = ((bf16[8,64,4,128]{3,1,2,0:T(8,128)(2,1)}), bf16[8,64,4,128]{3,1,2,0:T(8,128)(2,1)S(1)}, u32[]{:S(2)}, u32[]{:S(2)}) async-start(bf16[8,64,4,128]{3,1,2,0:T(8,128)(2,1)} %fusion.61), calls=%async_computation.1 | async-start | bytes 1048576 | tf_op jit(solution)/shard_map/all_to_all | solution.py:82
  107.7 0.2 fusion.49
  107.9 0.1 copy.113
  108.0 0.1 fusion.106
  108.1 0.3 copy.123
  108.4 0.3 copy.124
  108.8 8.4 %all-to-all-done.1 = bf16[8,64,4,128]{3,1,2,0:T(8,128)(2,1)S(1)} async-done(((bf16[8,64,4,128]{3,1,2,0:T(8,128)(2,1)}), bf16[8,64,4,128]{3,1,2,0:T(8,128)(2,1)S(1)}, u32[]{:S(2)}, u32[]{:S(2)}) %all-to-all-start.1) | async-done | bytes 524320 | tf_op jit(solution)/shard_map/all_to_all | solution.py:82
  117.2 0.3 fusion.69
  117.5 0.6 fusion.47
  118.1 0.5 fusion.72
  118.6 0.2 constant_dynamic-update-slice_fusion
  118.8 0.5 fusion.67
  119.3 0.5 fusion.71
  119.9 0.4 slice_dynamic-update-slice_fusion.19
  120.3 0.8 slice_dynamic-update-slice_fusion.18
  121.1 0.9 slice_dynamic-update-slice_fusion.17
  122.0 0.9 slice_dynamic-update-slice_fusion.16
  122.8 0.9 slice_dynamic-update-slice_fusion.15
  123.7 0.3 slice_dynamic-update-slice_fusion
  124.0 0.7 fusion.4
  124.7 0.7 fusion.2
  125.4 0.7 fusion.6
  126.1 0.7 fusion
  126.8 1.0 fusion.41
  127.8 1.1 copy.137
  (38 shorter events, 0.4 us)
Async XLA Ops:
  0.0 29.1 %copy-start = (bf16[1,64,32,128]{3,2,1,0:T(8,128)(2,1)S(1)}, bf16[1,64,32,128]{3,2,1,0:T(8,128)(2,1)}, u32[]{:S(2)}) copy-start(bf16[1,64,32,128]{3,2,1,0:T(8,128)(2,1)} %param.7) | copy-start | bytes 1572868
  0.9 44.5 %collective-permute-start.7 = (s32[1,32,2]{1,2,0:T(2,128)S(1)}, s32[1,32,2]{1,2,0:T(2,128)S(1)}, u32[]{:S(2)}, u32[]{:S(2)}) collective-permute-start(s32[1,32,2]{1,2,0:T(2,128)S(1)} %copy.167), channel_id=1, source_target_pairs={{16,0},{32,16},{48,32},{64,48},{80,64},{96,80},{112,96},{128,112},... | collective-permute-start | bytes 776 | tf_op jit(solution)/shard_map/ppermute | solution.py:54
  17.2 28.3 %collective-permute-start.6 = (s32[1,32,2]{1,2,0:T(2,128)S(1)}, s32[1,32,2]{1,2,0:T(2,128)S(1)}, u32[]{:S(2)}, u32[]{:S(2)}) collective-permute-start(s32[1,32,2]{1,2,0:T(2,128)S(1)} %copy.166), channel_id=1, source_target_pairs={{0,16},{16,32},{32,48},{48,64},{64,80},{80,96},{96,112},{112,128},... | collective-permute-start | bytes 776 | tf_op jit(solution)/shard_map/ppermute | solution.py:53
  21.6 23.0 %copy-start.4 = (f32[64]{0:T(128)S(1)}, f32[64]{0:T(128)}, u32[]{:S(2)}) copy-start(f32[64]{0:T(128)} %param.9) | copy-start | bytes 772
  21.7 23.1 %copy-start.3 = (s32[1,32,128]{2,1,0:T(8,128)S(1)}, s32[1,32,128]{2,1,0:T(8,128)}, u32[]{:S(2)}) copy-start(s32[1,32,128]{2,1,0:T(8,128)} %param.8) | copy-start | bytes 49156
  21.7 23.1 %copy-start.1 = (bf16[5,64,5,64]{3,1,2,0:T(8,128)(2,1)S(1)}, bf16[5,64,5,64]{3,1,2,0:T(8,128)(2,1)}, u32[]{:S(2)}) copy-start(bf16[5,64,5,64]{3,1,2,0:T(8,128)(2,1)} %param.12) | copy-start | bytes 614404
  23.9 46.6 %all-to-all-start = ((bf16[1,64,32,128]{3,1,0,2:T(8,128)(2,1)}), bf16[1,64,32,128]{3,1,0,2:T(8,128)(2,1)S(1)}, u32[]{:S(2)}, u32[]{:S(2)}) async-start(bf16[1,64,32,128]{3,1,0,2:T(8,128)(2,1)} %fusion.70), calls=%async_computation | async-start | bytes 1048576 | tf_op jit(solution)/shard_map/all_to_all | solution.py:72
  29.1 39.8 %copy-start.2 = (bf16[5,8,8,8]{3,2,1,0:T(8,128)(2,1)S(1)}, bf16[5,8,8,8]{3,2,1,0:T(8,128)(2,1)}, u32[]{:S(2)}) copy-start(bf16[5,8,8,8]{3,2,1,0:T(8,128)(2,1)} %param.10) | copy-start | bytes 15364
  29.8 15.6 %collective-permute-start.1 = (bf16[1,64,32,2]{2,1,3,0:T(8,128)(2,1)S(1)}, bf16[1,64,32,2]{2,1,3,0:T(8,128)(2,1)S(1)}, u32[]{:S(2)}, u32[]{:S(2)}) collective-permute-start(bf16[1,64,32,2]{2,1,3,0:T(8,128)(2,1)S(1)} %copy.160), channel_id=1, source_target_pairs={{16,0},{32,16},{48,32},{64,48},{80,64},{96,80},{112,96},{128,112},... | collective-permute-start | bytes 24584 | tf_op jit(solution)/shard_map/ppermute | solution.py:54
  42.7 14.8 %collective-permute-start = (bf16[1,64,32,2]{2,1,3,0:T(8,128)(2,1)S(1)}, bf16[1,64,32,2]{2,1,3,0:T(8,128)(2,1)S(1)}, u32[]{:S(2)}, u32[]{:S(2)}) collective-permute-start(bf16[1,64,32,2]{2,1,3,0:T(8,128)(2,1)S(1)} %copy.159), channel_id=1, source_target_pairs={{0,16},{16,32},{32,48},{48,64},{64,80},{80,96},{96,112},{112,128},... | collective-permute-start | bytes 24584 | tf_op jit(solution)/shard_map/ppermute | solution.py:53
  57.6 39.0 %collective-permute-start.5 = (bf16[1,64,32,4]{2,1,3,0:T(8,128)(2,1)S(1)}, bf16[1,64,32,4]{2,1,3,0:T(8,128)(2,1)S(1)}, u32[]{:S(2)}, u32[]{:S(2)}) collective-permute-start(bf16[1,64,32,4]{2,1,3,0:T(8,128)(2,1)S(1)} %fusion.85), channel_id=1, source_target_pairs={{2,0},{3,1},{4,2},{5,3},{6,4},{7,5},{8,6},{9,7},{10,8},{11,9},{12,... | collective-permute-start | bytes 49160 | tf_op jit(solution)/shard_map/ppermute | solution.py:45
  58.9 48.7 %collective-permute-start.4 = (bf16[1,64,32,4]{2,1,3,0:T(8,128)(2,1)S(1)}, bf16[1,64,32,4]{2,1,3,0:T(8,128)(2,1)S(1)}, u32[]{:S(2)}, u32[]{:S(2)}) collective-permute-start(bf16[1,64,32,4]{2,1,3,0:T(8,128)(2,1)S(1)} %fusion.85), channel_id=1, source_target_pairs={{1,0},{2,1},{3,2},{4,3},{5,4},{6,5},{7,6},{8,7},{9,8},{10,9},{11,1... | collective-permute-start | bytes 49160 | tf_op jit(solution)/shard_map/ppermute | solution.py:45
  62.7 6.5 %collective-permute-start.3 = (bf16[1,64,32,4]{2,1,3,0:T(8,128)(2,1)S(1)}, bf16[1,64,32,4]{2,1,3,0:T(8,128)(2,1)S(1)}, u32[]{:S(2)}, u32[]{:S(2)}) collective-permute-start(bf16[1,64,32,4]{2,1,3,0:T(8,128)(2,1)S(1)} %fusion.85), channel_id=1, source_target_pairs={{0,1},{1,2},{2,3},{3,4},{4,5},{5,6},{6,7},{7,8},{8,9},{9,10},{10,1... | collective-permute-start | bytes 49160 | tf_op jit(solution)/shard_map/ppermute | solution.py:45
  66.9 3.3 %collective-permute-start.2 = (bf16[1,64,32,4]{2,1,3,0:T(8,128)(2,1)S(1)}, bf16[1,64,32,4]{2,1,3,0:T(8,128)(2,1)S(1)}, u32[]{:S(2)}, u32[]{:S(2)}) collective-permute-start(bf16[1,64,32,4]{2,1,3,0:T(8,128)(2,1)S(1)} %fusion.85), channel_id=1, source_target_pairs={{0,2},{1,3},{2,4},{3,5},{4,6},{5,7},{6,8},{7,9},{8,10},{9,11},{10,... | collective-permute-start | bytes 49160 | tf_op jit(solution)/shard_map/ppermute | solution.py:45
  70.5 29.6 %collective-permute-start.8 = (bf16[2,64,4,128]{3,1,2,0:T(8,128)(2,1)S(1)}, bf16[2,64,4,128]{3,1,2,0:T(8,128)(2,1)S(1)}, u32[]{:S(2)}, u32[]{:S(2)}) collective-permute-start(bf16[2,64,4,128]{3,1,2,0:T(8,128)(2,1)S(1)} %fusion.86), channel_id=1, source_target_pairs={{0,8},{8,0},{1,9},{9,1},{2,10},{10,2},{3,11},{11,3},{4,12},{12,4},... | collective-permute-start | bytes 393224 | tf_op jit(solution)/shard_map/ppermute | solution.py:76
  101.4 0.7 copy-start.5
  103.3 13.8 %all-to-all-start.1 = ((bf16[8,64,4,128]{3,1,2,0:T(8,128)(2,1)}), bf16[8,64,4,128]{3,1,2,0:T(8,128)(2,1)S(1)}, u32[]{:S(2)}, u32[]{:S(2)}) async-start(bf16[8,64,4,128]{3,1,2,0:T(8,128)(2,1)} %fusion.61), calls=%async_computation.1 | async-start | bytes 1048576 | tf_op jit(solution)/shard_map/all_to_all | solution.py:82
  126.1 0.7 copy-start.6
where the time goes:
time: 130 us; the launch traced here: 129 us
  starting transfers between devices  79.3 us (61%)
  waiting for transfers between devices  24.5 us (19%)
  other arithmetic  9.11 us (7%)
  local copies, waits for them, and re-layouts  8.99 us (7%)
  matrix products  6.58 us (5%)
    ppermute x2, starting transfers between devices, lon_halo(): after = lax.ppermute(block[..., :width], 'lon', down)  28.5 us
    ppermute x1, starting transfers between devices, local(): recv = lax.ppermute(send, 'lat_hi', [(0, 1), (1, 0)])  26.1 us
    ppermute x2, waiting for transfers between devices, lon_halo(): before = lax.ppermute(block[..., length - width:], 'lon', up)  12 us
    ppermute x4, starting transfers between devices, shifted(): return lax.ppermute(block, axis, pairs)  11.3 us
    all_to_all x1, waiting for transfers between devices, local(): lax.all_to_all(vertical(taps, w_vert, b_vert), 'lat_lo', split_axis=0, co...  8.39 us
    all_to_all x1, starting transfers between devices, local(): lax.all_to_all(normed, 'lat_lo', split_axis=2, concat_axis=0, tiled=True)  5.25 us
    all_to_all x1, starting transfers between devices, local(): lax.all_to_all(vertical(taps, w_vert, b_vert), 'lat_lo', split_axis=0, co...  4.31 us
    unnamed x22, local copies, waits for them, and re-layouts  4.11 us
  transfers between devices with their start and end apart: 11, of which 4 were waited for; matrix products, arithmetic and copies ran while one was open for 9% of the time, Pallas kernels for 0%

commit v1 on v0

--- a/solution.py
+++ b/solution.py
@@ -69,7 +69,10 @@
     halo_mask = jnp.concatenate([mask_before, mask_after], axis=2)
     halo_masked = vertical(halo_taps, w_vert, b_vert) * halo_mask[:, None].astype(jnp.bfloat16)
     normed = normalize(fields, norm_gain)
-    columns = lax.all_to_all(normed, "lat_lo", split_axis=2, concat_axis=0, tiled=True)
+    columns = jnp.concatenate(
+        lax.all_to_all(jnp.stack(jnp.split(normed, lax.psum(1, "lat_lo"), axis=2)), "lat_lo", 0, 0),
+        axis=0,
+    )
     count_lev = columns.shape[0]
     upper = lax.axis_index("lat_hi") == 0
     send = jnp.where(upper, columns[count_lev - reach :], columns[:reach])

time: 130 us -> 134 us (1.031)
  local copies, waits for them, and re-layouts: 8.99 us -> 14.1 us
    unnamed x22 -> x29, local copies, waits for them, and re-layouts: 4.11 us -> 8.54 us
  transfers between devices with their start and end apart: 11 -> 11, of which waited for: 4 -> 4; matrix products, arithmetic and copies ran while one was open for 9% -> 12% of each run, Pallas kernels for 0% -> 0%
where the time goes in v1:
time: 134 us; the launch traced here: 133 us
  starting transfers between devices  79.3 us (59%)
  waiting for transfers between devices  24.5 us (18%)
  local copies, waits for them, and re-layouts  14.1 us (11%)
  other arithmetic  8.26 us (6%)
  matrix products  6.58 us (5%)
    ppermute x2, starting transfers between devices, lon_halo(): after = lax.ppermute(block[..., :width], 'lon', down)  28.5 us
    ppermute x1, starting transfers between devices, local(): recv = lax.ppermute(send, 'lat_hi', [(0, 1), (1, 0)])  26.1 us
    ppermute x2, waiting for transfers between devices, lon_halo(): before = lax.ppermute(block[..., length - width:], 'lon', up)  12 us
    ppermute x4, starting transfers between devices, shifted(): return lax.ppermute(block, axis, pairs)  11.3 us
    unnamed x29, local copies, waits for them, and re-layouts  8.54 us
    all_to_all x1, waiting for transfers between devices, local(): lax.all_to_all(vertical(taps, w_vert, b_vert), 'lat_lo', split_axis=0, co...  8.39 us
    all_to_all x1, starting transfers between devices, local(): lax.all_to_all(jnp.stack(jnp.split(normed, lax.psum(1, 'lat_lo'), axis=2)...  5.25 us
    all_to_all x1, starting transfers between devices, local(): lax.all_to_all(vertical(taps, w_vert, b_vert), 'lat_lo', split_axis=0, co...  4.31 us
  transfers between devices with their start and end apart: 11, of which 4 were waited for; matrix products, arithmetic and copies ran while one was open for 12% of the time, Pallas kernels for 0%

profile of v1, /device:TPU:1, one launch (start us, length us, event | category | flops | bytes accessed | tf_op | source)
XLA Modules:
  0.0 133.2 jit_solution(7585489422161689558)
XLA Ops:
  0.0 0.9 fusion.129
  0.9 16.2 %collective-permute-start.7 = (s32[1,32,2]{1,2,0:T(2,128)S(1)}, s32[1,32,2]{1,2,0:T(2,128)S(1)}, u32[]{:S(2)}, u32[]{:S(2)}) collective-permute-start(s32[1,32,2]{1,2,0:T(2,128)S(1)} %copy.173), channel_id=1, source_target_pairs={{16,0},{32,16},{48,32},{64,48},{80,64},{96,80},{112,96},{128,112},... | collective-permute-start | bytes 776 | tf_op jit(solution)/shard_map/ppermute | solution.py:54
  17.2 1.9 %collective-permute-start.6 = (s32[1,32,2]{1,2,0:T(2,128)S(1)}, s32[1,32,2]{1,2,0:T(2,128)S(1)}, u32[]{:S(2)}, u32[]{:S(2)}) collective-permute-start(s32[1,32,2]{1,2,0:T(2,128)S(1)} %copy.172), channel_id=1, source_target_pairs={{0,16},{16,32},{32,48},{48,64},{64,80},{80,96},{96,112},{112,128},... | collective-permute-start | bytes 776 | tf_op jit(solution)/shard_map/ppermute | solution.py:53
  19.1 1.2 convert_reduce_fusion
  20.3 1.3 fusion.51
  21.6 1.4 %fusion.53 = bf16[1,64,32,128]{3,1,2,0:T(8,128)(2,1)S(1)} fusion(f32[64]{0:T(128)} %param.9, f32[32,128]{1,0:T(8,128)S(1)} %add_rsqrt_fusion, f32[32,128]{1,0:T(8,128)S(1)} %broadcast_multiply_fusion, bf16[1,64,32,128]{3,2,1,0:T(8,128)(2,1)} %param.7), kind=kLoop, calls=%fused_computation.45 | loop fusion | flops 1310720 | bytes 1081600 | tf_op jit(solution)/shard_map/convert_element_type | solution.py:24
  23.0 0.6 constant_dynamic-update-slice_fusion.7
  23.6 0.6 constant_dynamic-update-slice_fusion.6
  24.3 0.6 constant_dynamic-update-slice_fusion.5
  24.9 0.6 constant_dynamic-update-slice_fusion.4
  25.5 0.6 constant_dynamic-update-slice_fusion.3
  26.2 0.6 constant_dynamic-update-slice_fusion.2
  26.8 0.6 constant_dynamic-update-slice_fusion.1
  27.4 0.6 constant_dynamic-update-slice_fusion
  28.1 5.3 %all-to-all-start = ((bf16[8,1,64,4,128]{4,2,3,1,0:T(8,128)(2,1)}), bf16[8,1,64,4,128]{4,2,3,1,0:T(8,128)(2,1)S(1)}, u32[]{:S(2)}, u32[]{:S(2)}) async-start(bf16[8,1,64,4,128]{4,2,3,1,0:T(8,128)(2,1)} %constant_dynamic-update-slice_fusion), calls=%async_computation | async-start | bytes 1048576 | tf_op jit(solution)/shard_map/all_to_all | solution.py:73
  33.3 0.2 fusion.126
  33.6 0.5 copy.166
  34.0 12.4 %collective-permute-start.1 = (bf16[1,64,32,2]{2,1,3,0:T(8,128)(2,1)S(1)}, bf16[1,64,32,2]{2,1,3,0:T(8,128)(2,1)S(1)}, u32[]{:S(2)}, u32[]{:S(2)}) collective-permute-start(bf16[1,64,32,2]{2,1,3,0:T(8,128)(2,1)S(1)} %copy.166), channel_id=1, source_target_pairs={{16,0},{32,16},{48,32},{64,48},{80,64},{96,80},{112,96},{128,112},... | collective-permute-start | bytes 24584 | tf_op jit(solution)/shard_map/ppermute | solution.py:54
  46.4 0.5 copy.165
  46.9 1.9 %collective-permute-start = (bf16[1,64,32,2]{2,1,3,0:T(8,128)(2,1)S(1)}, bf16[1,64,32,2]{2,1,3,0:T(8,128)(2,1)S(1)}, u32[]{:S(2)}, u32[]{:S(2)}) collective-permute-start(bf16[1,64,32,2]{2,1,3,0:T(8,128)(2,1)S(1)} %copy.165), channel_id=1, source_target_pairs={{0,16},{16,32},{32,48},{48,64},{64,80},{80,96},{96,112},{112,128},... | collective-permute-start | bytes 24584 | tf_op jit(solution)/shard_map/ppermute | solution.py:53
  49.1 0.1 copy.137
  49.2 0.1 copy.133
  49.7 12.0 %collective-permute-done = bf16[1,64,32,2]{2,1,3,0:T(8,128)(2,1)S(1)} collective-permute-done((bf16[1,64,32,2]{2,1,3,0:T(8,128)(2,1)S(1)}, bf16[1,64,32,2]{2,1,3,0:T(8,128)(2,1)S(1)}, u32[]{:S(2)}, u32[]{:S(2)}) %collective-permute-start) | collective-permute-done | bytes 8224 | tf_op jit(solution)/shard_map/ppermute | solution.py:53
  61.8 1.3 collective-permute-start.5
  63.1 3.8 %collective-permute-start.4 = (bf16[1,64,32,4]{2,1,3,0:T(8,128)(2,1)S(1)}, bf16[1,64,32,4]{2,1,3,0:T(8,128)(2,1)S(1)}, u32[]{:S(2)}, u32[]{:S(2)}) collective-permute-start(bf16[1,64,32,4]{2,1,3,0:T(8,128)(2,1)S(1)} %fusion.84), channel_id=1, source_target_pairs={{1,0},{2,1},{3,2},{4,3},{5,4},{6,5},{7,6},{8,7},{9,8},{10,9},{11,1... | collective-permute-start | bytes 49160 | tf_op jit(solution)/shard_map/ppermute | solution.py:45
  66.9 4.2 %collective-permute-start.3 = (bf16[1,64,32,4]{2,1,3,0:T(8,128)(2,1)S(1)}, bf16[1,64,32,4]{2,1,3,0:T(8,128)(2,1)S(1)}, u32[]{:S(2)}, u32[]{:S(2)}) collective-permute-start(bf16[1,64,32,4]{2,1,3,0:T(8,128)(2,1)S(1)} %fusion.84), channel_id=1, source_target_pairs={{0,1},{1,2},{2,3},{3,4},{4,5},{5,6},{6,7},{7,8},{8,9},{9,10},{10,1... | collective-permute-start | bytes 49160 | tf_op jit(solution)/shard_map/ppermute | solution.py:45
  71.1 2.0 %collective-permute-start.2 = (bf16[1,64,32,4]{2,1,3,0:T(8,128)(2,1)S(1)}, bf16[1,64,32,4]{2,1,3,0:T(8,128)(2,1)S(1)}, u32[]{:S(2)}, u32[]{:S(2)}) collective-permute-start(bf16[1,64,32,4]{2,1,3,0:T(8,128)(2,1)S(1)} %fusion.84), channel_id=1, source_target_pairs={{0,2},{1,3},{2,4},{3,5},{4,6},{5,7},{6,8},{7,9},{8,10},{9,11},{10,... | collective-permute-start | bytes 49160 | tf_op jit(solution)/shard_map/ppermute | solution.py:45
  73.1 0.2 fusion.94
  73.4 0.2 fusion.99
  73.6 0.9 collective-permute-done.2
  74.4 0.2 fusion.50
  74.7 26.1 %collective-permute-start.8 = (bf16[2,64,4,128]{3,1,2,0:T(8,128)(2,1)S(1)}, bf16[2,64,4,128]{3,1,2,0:T(8,128)(2,1)S(1)}, u32[]{:S(2)}, u32[]{:S(2)}) collective-permute-start(bf16[2,64,4,128]{3,1,2,0:T(8,128)(2,1)S(1)} %fusion.85), channel_id=1, source_target_pairs={{0,8},{8,0},{1,9},{9,1},{2,10},{10,2},{3,11},{11,3},{4,12},{12,4},... | collective-permute-start | bytes 393224 | tf_op jit(solution)/shard_map/ppermute | solution.py:79
  100.8 0.2 fusion.96
  101.0 3.3 %collective-permute-done.8 = bf16[2,64,4,128]{3,1,2,0:T(8,128)(2,1)S(1)} collective-permute-done((bf16[2,64,4,128]{3,1,2,0:T(8,128)(2,1)S(1)}, bf16[2,64,4,128]{3,1,2,0:T(8,128)(2,1)S(1)}, u32[]{:S(2)}, u32[]{:S(2)}) %collective-permute-start.8) | collective-permute-done | bytes 131104 | tf_op jit(solution)/shard_map/ppermute | solution.py:79
  104.3 0.1 fusion.72
  104.5 0.3 fusion.78
  104.8 0.3 convolution_add_fusion.3
  105.2 0.3 convolution_add_fusion.2
  105.6 0.4 convolution_add_fusion.1
  105.9 0.4 fusion.26
  106.3 1.2 fusion.61
  107.5 4.3 %all-to-all-start.1 = ((bf16[8,64,4,128]{3,1,2,0:T(8,128)(2,1)}), bf16[8,64,4,128]{3,1,2,0:T(8,128)(2,1)S(1)}, u32[]{:S(2)}, u32[]{:S(2)}) async-start(bf16[8,64,4,128]{3,1,2,0:T(8,128)(2,1)} %fusion.61), calls=%async_computation.1 | async-start | bytes 1048576 | tf_op jit(solution)/shard_map/all_to_all | solution.py:85
  111.9 0.2 fusion.49
  112.3 0.3 copy.129
  112.6 0.3 copy.130
  113.0 8.4 %all-to-all-done.1 = bf16[8,64,4,128]{3,1,2,0:T(8,128)(2,1)S(1)} async-done(((bf16[8,64,4,128]{3,1,2,0:T(8,128)(2,1)}), bf16[8,64,4,128]{3,1,2,0:T(8,128)(2,1)S(1)}, u32[]{:S(2)}, u32[]{:S(2)}) %all-to-all-start.1) | async-done | bytes 524320 | tf_op jit(solution)/shard_map/all_to_all | solution.py:85
  121.4 0.3 fusion.69
  121.7 0.6 fusion.47
  122.3 0.5 fusion.71
  122.8 0.2 constant_dynamic-update-slice_fusion.8
  123.0 0.5 fusion.67
  123.6 0.5 fusion.70
  124.1 0.4 slice_dynamic-update-slice_fusion.19
  124.5 0.8 slice_dynamic-update-slice_fusion.18
  125.3 0.9 slice_dynamic-update-slice_fusion.17
  126.2 0.9 slice_dynamic-update-slice_fusion.16
  127.0 0.9 slice_dynamic-update-slice_fusion.15
  127.9 0.3 slice_dynamic-update-slice_fusion
  128.2 0.7 fusion.4
  128.9 0.7 fusion.2
  129.6 0.7 fusion.6
  130.3 0.7 fusion
  131.0 1.0 fusion.41
  132.0 1.1 copy.143
  (46 shorter events, 1.2 us)
Async XLA Ops:
  0.0 33.3 %copy-start = (bf16[1,64,32,128]{3,2,1,0:T(8,128)(2,1)S(1)}, bf16[1,64,32,128]{3,2,1,0:T(8,128)(2,1)}, u32[]{:S(2)}) copy-start(bf16[1,64,32,128]{3,2,1,0:T(8,128)(2,1)} %param.7) | copy-start | bytes 1572868
  0.9 48.7 %collective-permute-start.7 = (s32[1,32,2]{1,2,0:T(2,128)S(1)}, s32[1,32,2]{1,2,0:T(2,128)S(1)}, u32[]{:S(2)}, u32[]{:S(2)}) collective-permute-start(s32[1,32,2]{1,2,0:T(2,128)S(1)} %copy.173), channel_id=1, source_target_pairs={{16,0},{32,16},{48,32},{64,48},{80,64},{96,80},{112,96},{128,112},... | collective-permute-start | bytes 776 | tf_op jit(solution)/shard_map/ppermute | solution.py:54
  17.2 32.5 %collective-permute-start.6 = (s32[1,32,2]{1,2,0:T(2,128)S(1)}, s32[1,32,2]{1,2,0:T(2,128)S(1)}, u32[]{:S(2)}, u32[]{:S(2)}) collective-permute-start(s32[1,32,2]{1,2,0:T(2,128)S(1)} %copy.172), channel_id=1, source_target_pairs={{0,16},{16,32},{32,48},{48,64},{64,80},{80,96},{96,112},{112,128},... | collective-permute-start | bytes 776 | tf_op jit(solution)/shard_map/ppermute | solution.py:53
  23.6 25.2 %copy-start.4 = (f32[64]{0:T(128)S(1)}, f32[64]{0:T(128)}, u32[]{:S(2)}) copy-start(f32[64]{0:T(128)} %param.9) | copy-start | bytes 772
  23.6 25.3 %copy-start.3 = (s32[1,32,128]{2,1,0:T(8,128)S(1)}, s32[1,32,128]{2,1,0:T(8,128)}, u32[]{:S(2)}) copy-start(s32[1,32,128]{2,1,0:T(8,128)} %param.8) | copy-start | bytes 49156
  23.6 25.3 %copy-start.1 = (bf16[5,64,5,64]{3,1,2,0:T(8,128)(2,1)S(1)}, bf16[5,64,5,64]{3,1,2,0:T(8,128)(2,1)}, u32[]{:S(2)}) copy-start(bf16[5,64,5,64]{3,1,2,0:T(8,128)(2,1)} %param.12) | copy-start | bytes 614404
  28.1 46.6 %all-to-all-start = ((bf16[8,1,64,4,128]{4,2,3,1,0:T(8,128)(2,1)}), bf16[8,1,64,4,128]{4,2,3,1,0:T(8,128)(2,1)S(1)}, u32[]{:S(2)}, u32[]{:S(2)}) async-start(bf16[8,1,64,4,128]{4,2,3,1,0:T(8,128)(2,1)} %constant_dynamic-update-slice_fusion), calls=%async_computation | async-start | bytes 1048576 | tf_op jit(solution)/shard_map/all_to_all | solution.py:73
  33.3 39.8 %copy-start.2 = (bf16[5,8,8,8]{3,2,1,0:T(8,128)(2,1)S(1)}, bf16[5,8,8,8]{3,2,1,0:T(8,128)(2,1)}, u32[]{:S(2)}) copy-start(bf16[5,8,8,8]{3,2,1,0:T(8,128)(2,1)} %param.10) | copy-start | bytes 15364
  34.0 15.6 %collective-permute-start.1 = (bf16[1,64,32,2]{2,1,3,0:T(8,128)(2,1)S(1)}, bf16[1,64,32,2]{2,1,3,0:T(8,128)(2,1)S(1)}, u32[]{:S(2)}, u32[]{:S(2)}) collective-permute-start(bf16[1,64,32,2]{2,1,3,0:T(8,128)(2,1)S(1)} %copy.166), channel_id=1, source_target_pairs={{16,0},{32,16},{48,32},{64,48},{80,64},{96,80},{112,96},{128,112},... | collective-permute-start | bytes 24584 | tf_op jit(solution)/shard_map/ppermute | solution.py:54
  46.9 14.8 %collective-permute-start = (bf16[1,64,32,2]{2,1,3,0:T(8,128)(2,1)S(1)}, bf16[1,64,32,2]{2,1,3,0:T(8,128)(2,1)S(1)}, u32[]{:S(2)}, u32[]{:S(2)}) collective-permute-start(bf16[1,64,32,2]{2,1,3,0:T(8,128)(2,1)S(1)} %copy.165), channel_id=1, source_target_pairs={{0,16},{16,32},{32,48},{48,64},{64,80},{80,96},{96,112},{112,128},... | collective-permute-start | bytes 24584 | tf_op jit(solution)/shard_map/ppermute | solution.py:53
  61.8 39.0 %collective-permute-start.5 = (bf16[1,64,32,4]{2,1,3,0:T(8,128)(2,1)S(1)}, bf16[1,64,32,4]{2,1,3,0:T(8,128)(2,1)S(1)}, u32[]{:S(2)}, u32[]{:S(2)}) collective-permute-start(bf16[1,64,32,4]{2,1,3,0:T(8,128)(2,1)S(1)} %fusion.84), channel_id=1, source_target_pairs={{2,0},{3,1},{4,2},{5,3},{6,4},{7,5},{8,6},{9,7},{10,8},{11,9},{12,... | collective-permute-start | bytes 49160 | tf_op jit(solution)/shard_map/ppermute | solution.py:45
  63.1 48.7 %collective-permute-start.4 = (bf16[1,64,32,4]{2,1,3,0:T(8,128)(2,1)S(1)}, bf16[1,64,32,4]{2,1,3,0:T(8,128)(2,1)S(1)}, u32[]{:S(2)}, u32[]{:S(2)}) collective-permute-start(bf16[1,64,32,4]{2,1,3,0:T(8,128)(2,1)S(1)} %fusion.84), channel_id=1, source_target_pairs={{1,0},{2,1},{3,2},{4,3},{5,4},{6,5},{7,6},{8,7},{9,8},{10,9},{11,1... | collective-permute-start | bytes 49160 | tf_op jit(solution)/shard_map/ppermute | solution.py:45
  66.9 6.5 %collective-permute-start.3 = (bf16[1,64,32,4]{2,1,3,0:T(8,128)(2,1)S(1)}, bf16[1,64,32,4]{2,1,3,0:T(8,128)(2,1)S(1)}, u32[]{:S(2)}, u32[]{:S(2)}) collective-permute-start(bf16[1,64,32,4]{2,1,3,0:T(8,128)(2,1)S(1)} %fusion.84), channel_id=1, source_target_pairs={{0,1},{1,2},{2,3},{3,4},{4,5},{5,6},{6,7},{7,8},{8,9},{9,10},{10,1... | collective-permute-start | bytes 49160 | tf_op jit(solution)/shard_map/ppermute | solution.py:45
  71.1 3.3 %collective-permute-start.2 = (bf16[1,64,32,4]{2,1,3,0:T(8,128)(2,1)S(1)}, bf16[1,64,32,4]{2,1,3,0:T(8,128)(2,1)S(1)}, u32[]{:S(2)}, u32[]{:S(2)}) collective-permute-start(bf16[1,64,32,4]{2,1,3,0:T(8,128)(2,1)S(1)} %fusion.84), channel_id=1, source_target_pairs={{0,2},{1,3},{2,4},{3,5},{4,6},{5,7},{6,8},{7,9},{8,10},{9,11},{10,... | collective-permute-start | bytes 49160 | tf_op jit(solution)/shard_map/ppermute | solution.py:45
  74.7 29.6 %collective-permute-start.8 = (bf16[2,64,4,128]{3,1,2,0:T(8,128)(2,1)S(1)}, bf16[2,64,4,128]{3,1,2,0:T(8,128)(2,1)S(1)}, u32[]{:S(2)}, u32[]{:S(2)}) collective-permute-start(bf16[2,64,4,128]{3,1,2,0:T(8,128)(2,1)S(1)} %fusion.85), channel_id=1, source_target_pairs={{0,8},{8,0},{1,9},{9,1},{2,10},{10,2},{3,11},{11,3},{4,12},{12,4},... | collective-permute-start | bytes 393224 | tf_op jit(solution)/shard_map/ppermute | solution.py:79
  105.6 0.7 copy-start.5
  107.5 13.8 %all-to-all-start.1 = ((bf16[8,64,4,128]{3,1,2,0:T(8,128)(2,1)}), bf16[8,64,4,128]{3,1,2,0:T(8,128)(2,1)S(1)}, u32[]{:S(2)}, u32[]{:S(2)}) async-start(bf16[8,64,4,128]{3,1,2,0:T(8,128)(2,1)} %fusion.61), calls=%async_computation.1 | async-start | bytes 1048576 | tf_op jit(solution)/shard_map/all_to_all | solution.py:85
  130.3 0.7 copy-start.6
